TPU v7x, 512 devices: a whole 4x4x16 slice. The times are simulated.
512 devices in a mesh: pack: 16 (over y, x), seq: 32 (over z, core).
Axes of the slice: x: 4, y: 4, z: 16, core: 2. Of those that a mesh axis runs over, the one named last changes fastest.
Arguments:
- queries: bfloat16 [65536, 2048], P(('pack', 'seq')), parts along dimension 0, may hold values from -48 to 48
- token_key_heads: bfloat16 [65536, 256], P(('pack', 'seq')), parts along dimension 0, may hold values from -6 to 6
- token_value_heads: bfloat16 [65536, 256], P(('pack', 'seq')), parts along dimension 0, may hold values from -6 to 6
- residual: bfloat16 [65536, 1024], P(('pack', 'seq')), parts along dimension 0, may hold values from -40 to 40
- out_weight: bfloat16 [2048, 1024], P('seq'), may hold values from -0.125 to 0.125
- norm_gain: bfloat16 [1024], replicated, may hold values from 0.5 to 1.5
- w_gate: bfloat16 [32, 1024, 384], P('seq'), may hold values from -0.1875 to 0.1875
- w_up: bfloat16 [32, 1024, 384], P('seq'), may hold values from -0.1875 to 0.1875
- w_down: bfloat16 [32, 384, 1024], P('seq'), may hold values from -0.3125 to 0.3125
- expert_ids: int32 [65536, 8], P(('pack', 'seq')), parts along dimension 0, may hold values from 0 to 31, all different within a row; in each aligned block of 128 rows (0 to 127, 128 to 255, ...) at most 48 rows name the same one
- gate_weights: float32 [65536, 8], P(('pack', 'seq')), parts along dimension 0, may hold values from 0.05 to 0.3
- doc_of_block: int32 [512], P('pack'), parts along dimension 0, may hold values from 0 to 7, never falling along the last dimension, each value on 1 to 8 neighbouring positions
Outputs:
- attention: bfloat16 [65536, 2048], P(('pack', 'seq')), parts along dimension 0
- hidden_out: bfloat16 [65536, 1024], P(('pack', 'seq')), parts along dimension 0
- expert_mix: bfloat16 [65536, 1024], P(('pack', 'seq')), parts along dimension 0
There are 16 independent parts, one for each index of `pack`. A program takes and returns all parts, laid end to end along the dimension named above; an argument that names none is the same for every part. Nothing has to cross between parts.
Inputs may be any that keep to these rules, and one draw needn't show every extreme that they name: `expert_ids`: each row names 8 different experts; within the rows of one block no expert is named more than 48 times, and in every draw some expert is named exactly 48 times by the rows of some block. `doc_of_block`: never falls from block to block; each document covers 1 to 8 blocks, one exactly 8.
All inputs are finite; a program needn't handle non-finite values.
Results may differ from a plain program's by a relative error of at most 0.015.
Values may be sent and summed in bfloat16 or wider, within the bound.
A program may use at most 64 MiB of HBM per device.

v0:
```python
import math
import jax
import jax.numpy as jnp
from jax import lax
from jax.sharding import PartitionSpec as P

QUERY_HEADS = 16
KEY_VALUE_HEADS = 2
HEAD_SIZE = 128
TOP = 8


def attend(queries, key_token_rows, value_token_rows, query_pos, key_pos, allowed):
    token_rows = queries.shape[0]
    heads_per_group = QUERY_HEADS // KEY_VALUE_HEADS
    token_query_heads = queries.reshape(token_rows, KEY_VALUE_HEADS, heads_per_group, HEAD_SIZE)
    key_count = key_token_rows.shape[0]
    tile_length = math.gcd(key_count, 512)
    number_of_tiles = key_count // tile_length
    key_tile_list = key_token_rows.reshape(number_of_tiles, tile_length, KEY_VALUE_HEADS, HEAD_SIZE)
    value_tile_list = value_token_rows.reshape(
        number_of_tiles, tile_length, KEY_VALUE_HEADS, HEAD_SIZE
    )
    pos_tiles = key_pos.reshape(number_of_tiles, tile_length)
    allowed_tiles = allowed.reshape(number_of_tiles, tile_length)
    factor = 1.0 / HEAD_SIZE**0.5

    def tile_step(running, tile):
        key_tile, value_tile, pos_tile, allowed_tile = tile
        visible = allowed_tile[None, :] & (pos_tile[None, :] <= query_pos[:, None])

        def compute(current):
            run_max, run_sum, accum = current
            scores = (
                jnp.einsum(
                    "tkgd,skd->kgts",
                    token_query_heads,
                    key_tile,
                    preferred_element_type=jnp.float32,
                )
                * factor
            )
            scores = jnp.where(visible, scores, -1e30)
            new_max = jnp.maximum(run_max, jnp.max(scores, axis=-1))
            terms = jnp.where(visible, jnp.exp(scores - new_max[..., None]), 0.0)
            rescale = jnp.exp(run_max - new_max)
            new_sum = run_sum * rescale + jnp.sum(terms, axis=-1)
            product = jnp.einsum(
                "kgts,skd->kgtd",
                terms.astype(jnp.bfloat16),
                value_tile,
                preferred_element_type=jnp.float32,
            )
            return (new_max, new_sum, accum * rescale[..., None] + product)

        return (lax.cond(jnp.any(visible), compute, lambda current: current, running), None)

    start_state = (
        jnp.full((KEY_VALUE_HEADS, heads_per_group, token_rows), -1e30, jnp.float32),
        jnp.zeros((KEY_VALUE_HEADS, heads_per_group, token_rows), jnp.float32),
        jnp.zeros((KEY_VALUE_HEADS, heads_per_group, token_rows, HEAD_SIZE), jnp.float32),
    )
    final_state, _ = lax.scan(
        tile_step, start_state, (key_tile_list, value_tile_list, pos_tiles, allowed_tiles)
    )
    run_max, run_sum, accum = final_state
    result = accum / run_sum[..., None]
    return (
        jnp.transpose(result, (2, 0, 1, 3))
        .reshape(token_rows, QUERY_HEADS * HEAD_SIZE)
        .astype(jnp.bfloat16)
    )


def expert_rows(arrived, gate_proj, up_proj, down_proj):
    sources, slot_count, width = arrived.shape
    flat_rows = arrived.reshape(sources * slot_count, width)
    gate_part = jnp.dot(flat_rows, gate_proj, preferred_element_type=jnp.float32)
    up_part = jnp.dot(flat_rows, up_proj, preferred_element_type=jnp.float32)
    activated = (jax.nn.silu(gate_part) * up_part).astype(jnp.bfloat16)
    produced = jnp.dot(activated, down_proj, preferred_element_type=jnp.float32).astype(
        jnp.bfloat16
    )
    return produced.reshape(sources, slot_count, width)


def shards(
    queries,
    token_key_heads,
    token_value_heads,
    residual,
    out_weight,
    norm_gain,
    w_gate,
    w_up,
    w_down,
    expert_ids,
    gate_weights,
    doc_of_block,
):
    token_rows = queries.shape[0]
    blocks = lax.axis_size("seq")
    own_index = lax.axis_index("seq")
    local_pos = jnp.arange(token_rows, dtype=jnp.int32)
    query_pos = own_index * token_rows + local_pos
    own_doc = doc_of_block[own_index]
    key_head_width = token_key_heads.shape[1]
    key_token_rows, value_token_rows = (
        lax.all_gather(token_key_heads, "seq", axis=0, tiled=True),
        lax.all_gather(token_value_heads, "seq", axis=0, tiled=True),
    )
    key_pos = jnp.arange(blocks * token_rows, dtype=jnp.int32)
    key_block = key_pos // token_rows
    allowed = (key_block <= own_index) & ((doc_of_block[key_block] == own_doc) | (key_block == 0))
    key_token_rows = key_token_rows.reshape(
        key_token_rows.shape[0], KEY_VALUE_HEADS, key_head_width // KEY_VALUE_HEADS
    )
    value_token_rows = value_token_rows.reshape(
        value_token_rows.shape[0], KEY_VALUE_HEADS, key_head_width // KEY_VALUE_HEADS
    )
    attention = attend(queries, key_token_rows, value_token_rows, query_pos, key_pos, allowed)
    width = residual.shape[1]
    projected = jnp.dot(
        attention,
        lax.all_gather(out_weight, "seq", axis=0, tiled=True),
        preferred_element_type=jnp.float32,
    )
    hidden_state = residual.astype(jnp.float32) + projected
    mean_square = jnp.mean(hidden_state * hidden_state, axis=-1, keepdims=True)
    normed = (hidden_state * lax.rsqrt(mean_square + 1e-06) * norm_gain.astype(jnp.float32)).astype(
        jnp.bfloat16
    )
    slot_cap = min(token_rows, 3 * token_rows * TOP // (2 * blocks))
    routed_ids = expert_ids.reshape(-1)
    one_hot = (routed_ids[:, None] == jnp.arange(blocks, dtype=jnp.int32)[None, :]).astype(
        jnp.int32
    )
    earlier = jnp.cumsum(one_hot, axis=0) - one_hot
    slot_pos = jnp.sum(earlier * one_hot, axis=1)
    slot_index = routed_ids * slot_cap + slot_pos
    token_of = jnp.arange(token_rows * TOP, dtype=jnp.int32) // TOP
    outgoing = (
        jnp.zeros((blocks * slot_cap, width), jnp.bfloat16).at[slot_index].set(normed[token_of])
    )
    outgoing = outgoing.reshape(blocks, slot_cap, width)
    arrived = lax.all_to_all(outgoing, "seq", split_axis=0, concat_axis=0, tiled=True)
    served = expert_rows(arrived, w_gate[0], w_up[0], w_down[0])
    returned_rows = lax.all_to_all(served, "seq", split_axis=0, concat_axis=0, tiled=True)
    picked = returned_rows.reshape(blocks * slot_cap, width)[slot_index].astype(jnp.float32)
    weighted = picked * gate_weights.reshape(-1)[:, None]
    expert_mix = jnp.sum(weighted.reshape(token_rows, TOP, width), axis=1).astype(jnp.bfloat16)
    return (attention, hidden_state.astype(jnp.bfloat16), expert_mix)


def solution(mesh):
    in_specs = (
        P(("pack", "seq"), None),
        P(("pack", "seq"), None),
        P(("pack", "seq"), None),
        P(("pack", "seq"), None),
        P("seq", None),
        P(),
        P("seq", None, None),
        P("seq", None, None),
        P("seq", None, None),
        P(("pack", "seq"), None),
        P(("pack", "seq"), None),
        P("pack"),
    )
    out_specs = (P(("pack", "seq"), None), P(("pack", "seq"), None), P(("pack", "seq"), None))
    return jax.shard_map(shards, mesh=mesh, in_specs=in_specs, out_specs=out_specs, check_vma=False)
```

profile of v0, /device:TPU:4, one launch (start us, length us, event | category | flops | bytes accessed | tf_op | source)
XLA Modules:
  0.0 583.3 jit_solution(16247242193508925619)
XLA Ops:
  7.2 0.7 all-gather.4.cloned.1.call-update
  8.0 0.7 all-gather.6.cloned.1.call-update
  8.7 0.7 all-gather.8.cloned.1.call-update
  9.4 0.8 copy.27
  11.9 1.9 fusion.43
  13.8 2.1 fusion.42
  15.8 4.5 compare_select_fusion.1
  20.3 16.1 %select_compare_fusion = pred[4096]{0:T(1024)(128)(4,1)S(1)} fusion(pred[4096]{0:T(1024)(128)(4,1)S(1)} %compare_reduce_fusion, pred[4096]{0:T(1024)(128)(4,1)S(1)} %compare_reduce_fusion.1, pred[4096]{0:T(1024)(128)(4,1)S(1)} %compare_reduce_fusion.2, pred[4096]{0:T(1024)(128)(4,1)S(1)} %compare_reduce_fusion.3, ...), kind=kLoop, calls=%fused_computation.99 | loop fusion | flops 106496 | bytes 122984 | tf_op jit(solution)/shard_map/eq | solution.py:114
  36.4 1.3 copy.20
  37.8 0.3 copy.23
  38.1 0.7 convert_element_type.59
  38.8 9.0 %reduce-window.6 = s32[32,8,128]{2,1,0:T(8,128)S(1)} reduce-window(s32[32,8,128]{2,1,0:T(8,128)S(1)} %fusion.37, s32[]{:T(128)} %copy.62), window={size=1x1x128 pad=0_0x0_0x127_0}, to_apply=%region_7.8 | reduce-window | flops 4161536 | bytes 262148 | tf_op jit(solution)/shard_map/reduce-window
  47.9 0.1 copy.29
  48.1 0.1 copy.26
  48.6 37.9 %all-gather.4.cloned.1.call-done = bf16[4096,256]{1,0:T(8,128)(2,1)} async-done(((bf16[128,256]{1,0:T(8,128)(2,1)}), bf16[4096,256]{1,0:T(8,128)(2,1)}) %all-gather.4.cloned.1.call-update) | async-done | bytes 2097168 | tf_op jit(solution)/shard_map/all_gather | solution.py:109
  86.5 2.5 reshape.356
  89.0 1.8 copy.22
  90.8 66.5 %all-gather.6.cloned.1.call-done = bf16[4096,256]{1,0:T(8,128)(2,1)} async-done(((bf16[128,256]{1,0:T(8,128)(2,1)}), bf16[4096,256]{1,0:T(8,128)(2,1)}) %all-gather.6.cloned.1.call-update) | async-done | bytes 2097168 | tf_op jit(solution)/shard_map/all_gather | solution.py:110
  157.3 2.5 reshape.357
  159.9 1.8 copy.24
  161.7 18.0 %while.15 = (s32[]{:T(128)}, f32[2,8,128]{2,1,0:T(8,128)S(1)}, f32[2,8,128]{2,1,0:T(8,128)S(1)}, f32[2,8,128,128]{3,2,1,0:T(8,128)S(1)}, pred[8,512]{1,0:T(8,128...) while((s32[]{:T(128)}, f32[2,8,128]{2,1,0:T(8,128)S(1)}, ...), condition=%wide.region_6.7_spmd.clone, body=%wide.region_0.6_spmd.clone.sunk | while | flops 551227520 | bytes 16131831 | solution.py:63
  161.8 0.8 compare_and_fusion.2
  163.3 5.4 conditional.3
  163.3 1.7 fusion.2
  165.0 1.0 fusion.4
  166.0 2.6 fusion.8
  168.8 0.8 compare_and_fusion.2
  170.4 0.8 compare_and_fusion.2
  171.9 0.8 compare_and_fusion.2
  173.5 0.8 compare_and_fusion.2
  175.1 0.8 compare_and_fusion.2
  176.7 0.8 compare_and_fusion.2
  178.3 0.8 compare_and_fusion.2
  179.8 0.3 fusion.33
  180.1 0.3 copy.25
  180.5 0.1 copy.43
  180.7 49.5 %all-gather.8.cloned.1.call-done = bf16[2048,1024]{1,0:T(8,128)(2,1)} async-done(((bf16[64,1024]{1,0:T(8,128)(2,1)}), bf16[2048,1024]{1,0:T(8,128)(2,1)}) %all-gather.8.cloned.1.call-update) | async-done | bytes 4194320 | tf_op jit(solution)/shard_map/all_gather | solution.py:125
  230.1 3.0 multiply_reduce_fusion
  233.2 0.8 multiply_convert_fusion
  233.9 14.9 %scatter_custom_fusion = bf16[1536,1024]{1,0:T(8,128)(2,1)} fusion(s32[1024]{0:T(1024)S(1)} %bitcast.128, bf16[128,1024]{1,0:T(8,128)(2,1)S(1)} %get-tuple-element.196, s32[1024]{0:T(1024)S(1)} %broadcast_clamp_fusion.1, bf16[]{:T(256)} %constant.107.clone.1), kind=kCustom, calls=%fused_computation.34 | custom fusion | bytes 3145730 | tf_op jit(solution)/shard_map/scatter | solution.py:143
  248.9 154.5 %all_to_all.10 = bf16[32,48,1024]{2,1,0:T(8,128)(2,1)S(1)} all-to-all(bf16[32,48,1024]{2,1,0:T(8,128)(2,1)} %bitcast.115), channel_id=1, replica_groups=mesh['pack'=16,'seq'=32] {'seq'}, dimensions={0} | all-to-all | bytes 6291456 | tf_op jit(solution)/shard_map/all_to_all | solution.py:146
  403.4 1.7 copy-done.1
  405.1 3.2 fusion.31
  408.3 7.8 %convolution_convert_fusion = bf16[1536,1024]{1,0:T(8,128)(2,1)} fusion(bf16[1536,1024]{1,0:T(8,128)(2,1)} %bitcast.118, f32[1536,384]{1,0:T(8,128)} %fusion.31, bf16[1,384,1024]{2,1,0:T(8,128)(2,1)S(1)} %copy-done, bf16[1,1024,384]{2,1,0:T(8,128)(2,1)S(1)} %copy-done.7), kind=kOutput, calls=%fused_computation.31 | convolution fusion | flops 2421030912 | bytes 10223616 | tf_op jit(solution)/shard_map/dot_general | solution.py:81
  416.1 4.9 all-to-all-start.1
  421.2 146.3 %all-to-all-done.1 = bf16[32,48,1024]{2,1,0:T(8,128)(2,1)} async-done(((bf16[32,48,1024]{2,1,0:T(8,128)(2,1)}), bf16[32,48,1024]{2,1,0:T(8,128)(2,1)}, u32[]{:S(2)}, u32[]{:S(2)}) %all-to-all-start.1) | async-done | bytes 3145760 | tf_op jit(solution)/shard_map/all_to_all | solution.py:148
  567.5 7.3 %gather_fusion = bf16[1024,1024]{1,0:T(8,128)(2,1)S(1)} fusion(bf16[1536,1024]{1,0:T(8,128)(2,1)} %bitcast.54, s32[1024]{0:T(1024)S(1)} %broadcast_clamp_fusion), kind=kCustom, calls=%fused_computation.1 | custom fusion | bytes 4198400 | tf_op jit(solution)/shard_map/gather | solution.py:149
  574.8 2.0 fusion.22
  (100 shorter events, 2.9 us)
Async XLA Ops:
  7.2 401.2 %copy-start = (bf16[1,384,1024]{2,1,0:T(8,128)(2,1)S(1)}, bf16[1,384,1024]{2,1,0:T(8,128)(2,1)}, u32[]{:S(2)}) copy-start(bf16[1,384,1024]{2,1,0:T(8,128)(2,1)} %param.24) | copy-start | bytes 2359300
  7.2 40.9 %copy-start.4 = (s32[128,8]{0,1:T(8,128)S(1)}, s32[128,8]{0,1:T(8,128)}, u32[]{:S(2)}) copy-start(s32[128,8]{0,1:T(8,128)} %param.25) | copy-start | bytes 12292
  7.2 79.3 %all-gather.4.cloned.1.call-start = ((), (), s32[]{:S(2)}) async-start(), calls=%async_computation.2 | async-start | bytes 2162688 | tf_op jit(solution)/shard_map/all_gather | solution.py:109
  7.9 149.4 %all-gather.6.cloned.1.call-start = ((), (), s32[]{:S(2)}) async-start(), calls=%async_computation.3 | async-start | bytes 2162688 | tf_op jit(solution)/shard_map/all_gather | solution.py:110
  8.7 221.5 %all-gather.8.cloned.1.call-start = ((), (), s32[]{:S(2)}) async-start(), calls=%async_computation.4 | async-start | bytes 4325376 | tf_op jit(solution)/shard_map/all_gather | solution.py:125
  179.8 50.4 %copy-start.3 = (bf16[128,1024]{1,0:T(8,128)(2,1)S(1)}, bf16[128,1024]{1,0:T(8,128)(2,1)}, u32[]{:S(2)}) copy-start(bf16[128,1024]{1,0:T(8,128)(2,1)} %param.19) | copy-start | bytes 786436
  180.6 53.3 %copy-start.2 = (bf16[16,8,16,128]{3,1,2,0:T(8,128)(2,1)}, bf16[16,8,16,128]{3,1,2,0:T(8,128)(2,1)S(1)}, u32[]{:S(2)}) copy-start(bf16[16,8,16,128]{3,1,2,0:T(8,128)(2,1)S(1)} %copy.43) | copy-start | bytes 1572868
  248.9 156.2 %copy-start.6 = (bf16[1,1024,384]{2,1,0:T(8,128)(2,1)S(1)}, bf16[1,1024,384]{2,1,0:T(8,128)(2,1)}, u32[]{:S(2)}) copy-start(bf16[1,1024,384]{2,1,0:T(8,128)(2,1)} %param.22) | copy-start | bytes 2359300
  403.4 1.7 copy-start.1
  405.1 3.3 copy-start.7
  416.1 5.0 copy-start.5
  416.1 151.3 %all-to-all-start.1 = ((bf16[32,48,1024]{2,1,0:T(8,128)(2,1)}), bf16[32,48,1024]{2,1,0:T(8,128)(2,1)}, u32[]{:S(2)}, u32[]{:S(2)}) async-start(bf16[32,48,1024]{2,1,0:T(8,128)(2,1)} %bitcast.116), calls=%async_computation.1 | async-start | bytes 6291456 | tf_op jit(solution)/shard_map/all_to_all | solution.py:148
Sparse Core Ops, SparseCore 0:
  10.1 76.2 all-gather.3
  88.6 68.6 all-gather.5
  159.4 70.6 all-gather.7
where the time goes:
time: 584 us; the launch traced here: 583 us
  waiting for transfers between devices  302 us (52%)
  blocking collectives  155 us (27%)
  other arithmetic  42.8 us (7%)
  local copies, waits for them, and re-layouts  40.6 us (7%)
  matrix products  18.4 us (3%)
  between operations  14 us (2%)
    all_to_all x1, blocking collectives, shards(): lax.all_to_all(outgoing, 'seq', split_axis=0, concat_axis=0, tiled=True)  155 us
    all_to_all x1, waiting for transfers between devices, shards(): lax.all_to_all(served, 'seq', split_axis=0, concat_axis=0, tiled=True)  146 us
    all_gather x1, waiting for transfers between devices, shards(): lax.all_gather(token_value_heads, 'seq', axis=0, tiled=True)  66.5 us
    all_gather x1, waiting for transfers between devices, shards(): lax.all_gather(out_weight, 'seq', axis=0, tiled=True)  49.5 us
    all_gather x1, waiting for transfers between devices, shards(): lax.all_gather(token_key_heads, 'seq', axis=0, tiled=True)  37.9 us
    eq x1, other arithmetic, shards(): doc_of_block[key_block] == own_doc  16.1 us
    scatter x1, local copies, waits for them, and re-layouts, shards(): jnp.zeros((blocks * slot_cap, width), jnp.bfloat16).at[slot_index]  14.9 us
  transfers between devices with their start and end apart: 4, of which 4 were waited for; matrix products, arithmetic and copies ran while one was open for 10% of the time, Pallas kernels for 0%

commit v1 on v0

--- a/solution.py
+++ b/solution.py
@@ -8,6 +8,11 @@
 KEY_VALUE_HEADS = 2
 HEAD_SIZE = 128
 TOP = 8
+
+
+def gather_from_all(x, axis, dim):
+    copies = jnp.concatenate([x] * lax.axis_size(axis), axis=dim)
+    return lax.all_to_all(copies, axis, dim, dim, tiled=True)
 
 
 def attend(queries, key_token_rows, value_token_rows, query_pos, key_pos, allowed):
@@ -107,7 +112,7 @@
     key_head_width = token_key_heads.shape[1]
     key_token_rows, value_token_rows = (
         lax.all_gather(token_key_heads, "seq", axis=0, tiled=True),
-        lax.all_gather(token_value_heads, "seq", axis=0, tiled=True),
+        gather_from_all(token_value_heads, "seq", 0),
     )
     key_pos = jnp.arange(blocks * token_rows, dtype=jnp.int32)
     key_block = key_pos // token_rows

time: 584 us -> 554 us (0.949)
  the two profiles are of different devices: /device:TPU:4 before, /device:TPU:12 now
where the time goes in v1:
time: 554 us; the launch traced here: 551 us
  waiting for transfers between devices  209 us (38%)
  blocking collectives  154 us (28%)
  local copies, waits for them, and re-layouts  74.6 us (13%)
  other arithmetic  54.2 us (10%)
  starting transfers between devices  20.6 us (4%)
  matrix products  18.4 us (3%)
  between operations  14.4 us (3%)
  loops' own time  5.58 us (1%)
    all_to_all x1, blocking collectives, shards(): lax.all_to_all(outgoing, 'seq', split_axis=0, concat_axis=0, tiled=True)  154 us
    all_to_all x1, waiting for transfers between devices, shards(): lax.all_to_all(served, 'seq', split_axis=0, concat_axis=0, tiled=True)  146 us
    all_to_all x1, waiting for transfers between devices, gather_from_all(): return lax.all_to_all(copies, axis, dim, dim, tiled=True)  24.4 us
    unnamed x64, local copies, waits for them, and re-layouts  24.3 us
    all_gather x1, waiting for transfers between devices, shards(): lax.all_gather(token_key_heads, 'seq', axis=0, tiled=True)  21.7 us
    eq x1, other arithmetic, shards(): doc_of_block[key_block] == own_doc  16.2 us
    another operation x3, other arithmetic  15.8 us
    all_to_all x1, starting transfers between devices, gather_from_all(): return lax.all_to_all(copies, axis, dim, dim, tiled=True)  15.6 us
  transfers between devices with their start and end apart: 4, of which 4 were waited for; matrix products, arithmetic and copies ran while one was open for 19% of the time, Pallas kernels for 0%

profile of v1, /device:TPU:12, one launch (start us, length us, event | category | flops | bytes accessed | tf_op | source)
XLA Modules:
  0.0 550.6 jit_solution(1828405874058859242)
XLA Ops:
  7.9 0.8 constant_dynamic-update-slice_fusion.31
  8.8 0.8 constant_dynamic-update-slice_fusion.30
  9.6 0.8 constant_dynamic-update-slice_fusion.29
  10.5 0.8 constant_dynamic-update-slice_fusion.28
  11.3 0.8 constant_dynamic-update-slice_fusion.27
  12.1 0.8 constant_dynamic-update-slice_fusion.26
  13.0 0.8 constant_dynamic-update-slice_fusion.25
  13.8 0.8 constant_dynamic-update-slice_fusion.24
  14.7 0.8 constant_dynamic-update-slice_fusion.23
  15.5 0.8 constant_dynamic-update-slice_fusion.22
  16.4 0.8 constant_dynamic-update-slice_fusion.21
  17.2 0.8 constant_dynamic-update-slice_fusion.20
  18.1 0.8 constant_dynamic-update-slice_fusion.19
  19.7 0.8 constant_dynamic-update-slice_fusion.17
  21.7 2.9 copy.49
  24.6 15.6 %all-to-all-start = ((bf16[32,128,256]{1,2,0:T(8,128)(2,1)}), bf16[32,128,256]{1,2,0:T(8,128)(2,1)S(1)}, u32[]{:S(2)}, u32[]{:S(2)}) async-start(bf16[32,128,256]{1,2,0:T(8,128)(2,1)} %copy.49), calls=%async_computation | async-start | bytes 4194304 | tf_op jit(solution)/shard_map/all_to_all | solution.py:15
  44.9 4.5 compare_select_fusion.1
  49.4 16.2 %select_compare_fusion = pred[4096]{0:T(1024)(128)(4,1)S(1)} fusion(pred[4096]{0:T(1024)(128)(4,1)S(1)} %compare_reduce_fusion, pred[4096]{0:T(1024)(128)(4,1)S(1)} %compare_reduce_fusion.1, pred[4096]{0:T(1024)(128)(4,1)S(1)} %compare_reduce_fusion.2, pred[4096]{0:T(1024)(128)(4,1)S(1)} %compare_reduce_fusion.3, ...), kind=kLoop, calls=%fused_computation.131 | loop fusion | flops 106496 | bytes 122984 | tf_op jit(solution)/shard_map/eq | solution.py:119
  66.2 1.0 copy.48
  67.2 1.3 copy.52
  69.8 15.7 %reduce-window.6 = s32[32,8,128]{2,1,0:T(8,128)S(1)} reduce-window(s32[32,8,128]{2,1,0:T(8,128)} %fusion.37, s32[]{:T(128)} %copy.120), window={size=1x1x128 pad=0_0x0_0x127_0}, to_apply=%region_7.8 | reduce-window | flops 4161536 | bytes 262148 | tf_op jit(solution)/shard_map/reduce-window
  86.2 1.0 copy.58
  88.6 1.3 broadcast_multiply_fusion
  89.9 1.4 copy.55
  91.3 1.5 mul.85
  95.7 21.7 %all-gather.3.cloned.1.call-done = bf16[4096,256]{1,0:T(8,128)(2,1)} async-done(((bf16[128,256]{1,0:T(8,128)(2,1)}), bf16[4096,256]{1,0:T(8,128)(2,1)}) %all-gather.3.cloned.1.call-update) | async-done | bytes 2097168 | tf_op jit(solution)/shard_map/all_gather | solution.py:114
  117.4 4.0 reshape.359
  121.4 3.4 copy.51
  124.8 24.4 %all-to-all-done = bf16[32,128,256]{1,2,0:T(8,128)(2,1)S(1)} async-done(((bf16[32,128,256]{1,2,0:T(8,128)(2,1)}), bf16[32,128,256]{1,2,0:T(8,128)(2,1)S(1)}, u32[]{:S(2)}, u32[]{:S(2)}) %all-to-all-start) | async-done | bytes 2097184 | tf_op jit(solution)/shard_map/all_to_all | solution.py:15
  149.2 2.7 copy.50
  151.9 3.1 reshape_reshape.7
  155.0 3.0 copy.53
  158.1 23.7 %while.15 = (s32[]{:T(128)}, f32[2,8,128]{2,1,0:T(8,128)S(1)}, f32[2,8,128]{2,1,0:T(8,128)S(1)}, f32[2,8,128,128]{3,2,1,0:T(8,128)S(1)}, pred[8,512]{1,0:T(8,128...) while((s32[]{:T(128)}, f32[2,8,128]{2,1,0:T(8,128)S(1)}, ...), condition=%wide.region_6.7_spmd.clone, body=%wide.region_0.6_spmd.clone.sunk | while | flops 551227520 | bytes 16131831 | solution.py:68
  160.4 5.4 conditional.3
  160.4 1.7 fusion.2
  162.1 1.0 fusion.4
  163.1 2.6 fusion.8
  182.7 15.1 %all-gather.5.cloned.1.call-done = bf16[2048,1024]{1,0:T(8,128)(2,1)} async-done(((bf16[64,1024]{1,0:T(8,128)(2,1)}), bf16[2048,1024]{1,0:T(8,128)(2,1)}) %all-gather.5.cloned.1.call-update) | async-done | bytes 4194320 | tf_op jit(solution)/shard_map/all_gather | solution.py:130
  197.7 3.0 multiply_reduce_fusion
  201.5 15.0 %scatter_custom_fusion = bf16[1536,1024]{1,0:T(8,128)(2,1)} fusion(s32[1024]{0:T(1024)S(1)} %bitcast.132, bf16[128,1024]{1,0:T(8,128)(2,1)S(1)} %get-tuple-element.216, s32[1024]{0:T(1024)S(1)} %broadcast_clamp_fusion.1, bf16[]{:T(256)} %constant.107.clone.1), kind=kCustom, calls=%fused_computation.34 | custom fusion | bytes 3145730 | tf_op jit(solution)/shard_map/scatter | solution.py:148
  216.5 153.9 %all_to_all.19 = bf16[32,48,1024]{2,1,0:T(8,128)(2,1)S(1)} all-to-all(bf16[32,48,1024]{2,1,0:T(8,128)(2,1)} %bitcast.118), channel_id=1, replica_groups=mesh['pack'=16,'seq'=32] {'seq'}, dimensions={0} | all-to-all | bytes 6291456 | tf_op jit(solution)/shard_map/all_to_all | solution.py:151
  370.4 1.7 copy-done.2
  372.1 3.3 fusion.31
  375.4 7.8 %convolution_convert_fusion = bf16[1536,1024]{1,0:T(8,128)(2,1)} fusion(bf16[1536,1024]{1,0:T(8,128)(2,1)} %bitcast.121, f32[1536,384]{1,0:T(8,128)} %fusion.31, bf16[1,384,1024]{2,1,0:T(8,128)(2,1)S(1)} %copy-done, bf16[1,1024,384]{2,1,0:T(8,128)(2,1)S(1)} %copy-done.12), kind=kOutput, calls=%fused_computation.31 | convolution fusion | flops 2421030912 | bytes 10223616 | tf_op jit(solution)/shard_map/dot_general | solution.py:86
  383.1 4.9 all-to-all-start.2
  388.2 146.3 %all-to-all-done.2 = bf16[32,48,1024]{2,1,0:T(8,128)(2,1)} async-done(((bf16[32,48,1024]{2,1,0:T(8,128)(2,1)}), bf16[32,48,1024]{2,1,0:T(8,128)(2,1)}, u32[]{:S(2)}, u32[]{:S(2)}) %all-to-all-start.2) | async-done | bytes 3145760 | tf_op jit(solution)/shard_map/all_to_all | solution.py:153
  534.5 7.3 %gather_fusion = bf16[1024,1024]{1,0:T(8,128)(2,1)S(1)} fusion(bf16[1536,1024]{1,0:T(8,128)(2,1)} %bitcast.55, s32[1024]{0:T(1024)S(1)} %broadcast_clamp_fusion), kind=kCustom, calls=%fused_computation.1 | custom fusion | bytes 4198400 | tf_op jit(solution)/shard_map/gather | solution.py:154
  541.8 2.0 fusion.22
  (143 shorter events, 28.7 us)
Async XLA Ops:
  7.2 368.2 %copy-start = (bf16[1,384,1024]{2,1,0:T(8,128)(2,1)S(1)}, bf16[1,384,1024]{2,1,0:T(8,128)(2,1)}, u32[]{:S(2)}) copy-start(bf16[1,384,1024]{2,1,0:T(8,128)(2,1)} %param.24) | copy-start | bytes 2359300
  7.2 14.3 %copy-start.1 = (bf16[128,256]{1,0:T(8,128)(2,1)S(1)}, bf16[128,256]{1,0:T(8,128)(2,1)}, u32[]{:S(2)}) copy-start(bf16[128,256]{1,0:T(8,128)(2,1)} %param.18) | copy-start | bytes 196612
  7.2 110.2 %all-gather.3.cloned.1.call-start = ((), (), s32[]{:S(2)}) async-start(), calls=%async_computation.3 | async-start | bytes 2162688 | tf_op jit(solution)/shard_map/all_gather | solution.py:114
  24.6 16.4 %copy-start.8 = (s32[128,8]{0,1:T(8,128)S(1)}, s32[128,8]{0,1:T(8,128)}, u32[]{:S(2)}) copy-start(s32[128,8]{0,1:T(8,128)} %param.25) | copy-start | bytes 12292
  24.6 18.9 %copy-start.4 = (s32[32]{0:T(128)S(1)}, s32[32]{0:T(128)}, u32[]{:S(2)}) copy-start(s32[32]{0:T(128)} %param.27) | copy-start | bytes 388
  24.6 41.6 %copy-start.5 = (bf16[128,2048]{1,0:T(8,128)(2,1)S(1)}, bf16[128,2048]{1,0:T(8,128)(2,1)}, u32[]{:S(2)}) copy-start(bf16[128,2048]{1,0:T(8,128)(2,1)} %param.16) | copy-start | bytes 1572868
  24.6 124.7 %all-to-all-start = ((bf16[32,128,256]{1,2,0:T(8,128)(2,1)}), bf16[32,128,256]{1,2,0:T(8,128)(2,1)S(1)}, u32[]{:S(2)}, u32[]{:S(2)}) async-start(bf16[32,128,256]{1,2,0:T(8,128)(2,1)} %copy.49), calls=%async_computation | async-start | bytes 4194304 | tf_op jit(solution)/shard_map/all_to_all | solution.py:15
  40.2 28.3 %copy-start.10 = (bf16[1024]{0:T(1024)(128)(2,1)S(1)}, bf16[1024]{0:T(1024)(128)(2,1)}, u32[]{:S(2)}) copy-start(bf16[1024]{0:T(1024)(128)(2,1)} %param.21) | copy-start | bytes 6148
  40.2 157.5 %all-gather.5.cloned.1.call-start = ((), (), s32[]{:S(2)}) async-start(), calls=%async_computation.4 | async-start | bytes 4325376 | tf_op jit(solution)/shard_map/all_gather | solution.py:130
  181.8 15.9 %copy-start.6 = (bf16[128,1024]{1,0:T(8,128)(2,1)S(1)}, bf16[128,1024]{1,0:T(8,128)(2,1)}, u32[]{:S(2)}) copy-start(bf16[128,1024]{1,0:T(8,128)(2,1)} %param.19) | copy-start | bytes 786436
  182.7 18.1 %copy-start.3 = (bf16[16,8,16,128]{3,1,2,0:T(8,128)(2,1)}, bf16[16,8,16,128]{3,1,2,0:T(8,128)(2,1)S(1)}, u32[]{:S(2)}) copy-start(bf16[16,8,16,128]{3,1,2,0:T(8,128)(2,1)S(1)} %copy.70) | copy-start | bytes 1572868
  197.7 3.0 copy-start.7
  216.5 155.6 %copy-start.11 = (bf16[1,1024,384]{2,1,0:T(8,128)(2,1)S(1)}, bf16[1,1024,384]{2,1,0:T(8,128)(2,1)}, u32[]{:S(2)}) copy-start(bf16[1,1024,384]{2,1,0:T(8,128)(2,1)} %param.22) | copy-start | bytes 2359300
  370.4 1.7 copy-start.2
  372.1 3.3 copy-start.12
  383.1 5.0 copy-start.9
  383.1 151.3 %all-to-all-start.2 = ((bf16[32,48,1024]{2,1,0:T(8,128)(2,1)}), bf16[32,48,1024]{2,1,0:T(8,128)(2,1)}, u32[]{:S(2)}, u32[]{:S(2)}) async-start(bf16[32,48,1024]{2,1,0:T(8,128)(2,1)} %bitcast.119), calls=%async_computation.2 | async-start | bytes 6291456 | tf_op jit(solution)/shard_map/all_to_all | solution.py:153
Sparse Core Ops, SparseCore 0:
  10.1 107.2 all-gather.2
  119.6 78.1 all-gather.4
